TPU v7x, 32 devices: a whole 2x2x4 slice. The times are simulated.
32 devices in a mesh: group: 4 (over y, x), member: 8 (over z, core).
Axes of the slice: x: 2, y: 2, z: 4, core: 2. Of those that a mesh axis runs over, the one named last changes fastest.
Arguments:
- activations: bfloat16 [4, 1024, 2048], P('group', 'member'), may hold values from -6 to 6
- lengths: int32 [4, 8], P('group'), may hold values from 1 to 128, 576 in all within a row
- assignment: int32 [4, 8], P('group'), may hold values from 0 to 7, each once within a row
- owners: int32 [4], replicated, may hold values from 0 to 3
- prefix_cache: bfloat16 [4, 8192, 256], P('group', 'member'), may hold values from -244 to 244
- first_gain: float32 [2048], replicated, may hold values from 0.1 to 1.9
- first_bias: float32 [2048], replicated, may hold values from -3 to 3
- query_weight: bfloat16 [2048, 2048], replicated, may hold values from -0.125 to 0.125
- keyval_weight: bfloat16 [2048, 256], replicated, may hold values from -0.4375 to 0.4375
- output_weight: bfloat16 [2048, 2048], replicated, may hold values from -0.125 to 0.125
- second_gain: float32 [2048], replicated, may hold values from 0.1 to 1.9
- second_bias: float32 [2048], replicated, may hold values from -3 to 3
- expand_weight: bfloat16 [2048, 8192], P(None, 'member'), may hold values from -0.125 to 0.125
- contract_weight: bfloat16 [8192, 2048], P('member'), may hold values from -0.0625 to 0.0625
Outputs:
- layer_output: bfloat16 [4, 1024, 2048], P('group', 'member')
Inputs may be any that keep to these rules, and one draw needn't show every extreme that they name: Each row of lengths sums to 576 and its longest entry is 128. Each row of assignment names every request of its group once. `owners`: several groups may attend the same cache slot.
All inputs are finite; a program needn't handle non-finite values.
Results may differ from a plain program's by a relative error of at most 0.011.
The roundings to bfloat16 on the way count: a program that leaves them out, or rounds other values in their place, can miss the bound.
Values may be sent and summed in bfloat16 or wider, within the bound.
No kernel may reach another device: no remote copies, remote signals or barrier semaphores. Data moves between devices by JAX's collectives and lax.ppermute only.
A program may use at most 128 MiB of HBM per device.

v0:
```python
import math
import jax
import jax.numpy as jnp
from jax import lax
from jax.sharding import PartitionSpec as P

EPSILON = 1e-05
NEGATIVE = -1e30


def layer_norm(values, gain, bias):
    average = jnp.mean(values, axis=-1, keepdims=True)
    centered = values - average
    spread = jnp.mean(centered * centered, axis=-1, keepdims=True)
    return centered * lax.rsqrt(spread + EPSILON) * gain + bias


def pick_value(table, wanted):
    slots_at = lax.broadcasted_iota(jnp.int32, table.shape, 0)
    return jnp.sum(jnp.where(slots_at == wanted, table, 0))


def own_scores(query_block, own_keys, scaling):
    scores = (
        jnp.einsum("thd,sd->ths", query_block, own_keys, preferred_element_type=jnp.float32)
        * scaling
    )
    block_rows = query_block.shape[0]
    key_rows = own_keys.shape[0]
    row_at = lax.broadcasted_iota(jnp.int32, (block_rows, 1, key_rows), 0)
    column_at = lax.broadcasted_iota(jnp.int32, (block_rows, 1, key_rows), 2)
    return jnp.where(column_at <= row_at, scores, NEGATIVE)


def folded_attention(queries, keys_values, selected):
    row_count, head_count, head_size = queries.shape
    scaling = 1.0 / math.sqrt(head_size)
    own_keys = keys_values[:, :head_size]
    own_values = keys_values[:, head_size:]
    suffix_scores = own_scores(queries, own_keys, scaling)
    highest = jnp.max(suffix_scores, axis=-1)
    suffix_exp = jnp.exp(suffix_scores - highest[..., None])
    denominator = jnp.sum(suffix_exp, axis=-1)
    weighted = jnp.einsum(
        "ths,sd->thd",
        suffix_exp.astype(jnp.bfloat16),
        own_values,
        preferred_element_type=jnp.float32,
    )
    running = (weighted, highest, denominator)
    portion = lax.all_gather(selected, "member", axis=0, tiled=True)
    extent = portion.shape[0]
    stride = math.gcd(extent, 1024)

    def advance(state_now, block_index):
        weighted_now, highest_now, denominator_now = state_now
        key_block = lax.dynamic_slice_in_dim(portion, block_index * stride, stride, 0)
        scores = (
            jnp.einsum(
                "thd,pd->thp", queries, key_block[:, :head_size], preferred_element_type=jnp.float32
            )
            * scaling
        )
        highest_next = jnp.maximum(highest_now, jnp.max(scores, axis=-1))
        rescale = jnp.exp(highest_now - highest_next)
        exponent = jnp.exp(scores - highest_next[..., None])
        denominator_next = denominator_now * rescale + jnp.sum(exponent, axis=-1)
        weighted_next = weighted_now * rescale[..., None] + jnp.einsum(
            "thp,pd->thd",
            exponent.astype(jnp.bfloat16),
            key_block[:, head_size:],
            preferred_element_type=jnp.float32,
        )
        return ((weighted_next, highest_next, denominator_next), None)

    running, _ = lax.scan(advance, running, jnp.arange(extent // stride, dtype=jnp.int32))
    weighted, highest, denominator = running
    return (
        (weighted / denominator[..., None])
        .astype(jnp.bfloat16)
        .reshape(row_count, head_count * head_size)
    )


def shards(
    activations,
    lengths,
    assignment,
    owners,
    prefix_cache,
    first_gain,
    first_bias,
    query_weight,
    keyval_weight,
    output_weight,
    second_gain,
    second_bias,
    expand_weight,
    contract_weight,
):
    group_index = lax.axis_index("group")
    member_index = lax.axis_index("member")
    request = pick_value(assignment[0], member_index)
    length_here = pick_value(lengths[0], request)
    owner_here = pick_value(owners, group_index)
    tokens = activations[0]
    row_count = tokens.shape[0]
    head_size = prefix_cache.shape[2] // 2
    head_count = tokens.shape[1] // head_size
    every_block = lax.all_gather(prefix_cache, "group", axis=0, tiled=True)
    selected = lax.dynamic_index_in_dim(every_block, owner_here, 0, keepdims=False)
    tokens_wide = tokens.astype(jnp.float32)
    normed = layer_norm(tokens_wide, first_gain, first_bias).astype(jnp.bfloat16)
    queries = jnp.dot(normed, query_weight, preferred_element_type=jnp.float32).astype(jnp.bfloat16)
    queries = queries.reshape(row_count, head_count, head_size)
    keys_values = jnp.dot(normed, keyval_weight, preferred_element_type=jnp.float32).astype(
        jnp.bfloat16
    )
    attended = folded_attention(queries, keys_values, selected)
    residual = tokens_wide + jnp.dot(attended, output_weight, preferred_element_type=jnp.float32)
    second = layer_norm(residual, second_gain, second_bias).astype(jnp.bfloat16)
    hidden = jax.nn.gelu(
        jnp.dot(
            lax.all_gather(second, "member", axis=0, tiled=True),
            expand_weight,
            preferred_element_type=jnp.float32,
        ),
        approximate=True,
    ).astype(jnp.bfloat16)
    summed = lax.psum_scatter(
        jnp.dot(hidden, contract_weight, preferred_element_type=jnp.float32).astype(jnp.bfloat16),
        "member",
        scatter_dimension=0,
        tiled=True,
    ).astype(jnp.float32)
    is_live = lax.broadcasted_iota(jnp.int32, (row_count, 1), 0) < length_here
    return jnp.where(is_live, residual + summed, 0.0).astype(jnp.bfloat16)[None]


def solution(mesh):
    return jax.shard_map(
        shards,
        mesh=mesh,
        in_specs=(
            P("group", "member", None),
            P("group", None),
            P("group", None),
            P(),
            P("group", "member", None),
            P(),
            P(),
            P(),
            P(),
            P(),
            P(),
            P(),
            P(None, "member"),
            P("member", None),
        ),
        out_specs=P("group", "member", None),
        check_vma=False,
    )
```

profile of v0, /device:TPU:0, one launch (start us, length us, event | category | flops | bytes accessed | tf_op | source)
XLA Modules:
  0.0 286.6 jit_solution(2638500522030421383)
XLA Ops:
  10.5 36.7 %all-gather.5.cloned.1.call-done = bf16[4,1024,256]{2,1,0:T(8,128)(2,1)} async-done(((bf16[1,1024,256]{2,1,0:T(8,128)(2,1)}), bf16[4,1024,256]{2,1,0:T(8,128)(2,1)}) %all-gather.5.cloned.1.call-update) | async-done | bytes 2097168 | tf_op jit(solution)/shard_map/all_gather | solution.py:110
  47.2 1.9 constant_dynamic-slice_fusion
  51.8 5.0 %fusion.30 = bf16[16,16,8,128]{3,2,1,0:T(8,128)(2,1)S(1)} fusion(bf16[2048,2048]{1,0:T(8,128)(2,1)} %param.23, bf16[1,128,2048]{2,1,0:T(8,128)(2,1)} %param.16, f32[2048]{0:T(1024)} %param.22, f32[2048]{0:T(1024)} %param.21, f32[128]{0:T(128)S(1)} %add_rsqrt_fusion.1, f32[128]{0:T(128)S(1)} %broadcast_multiply_fusion.1), kind=kOutput, calls=%fused_computation.39 | convolution fusion | flops 1075576832 | bytes 9454592 | tf_op jit(solution)/shard_map/dot_general | solution.py:114
  58.2 38.3 %all-gather.9.cloned.1.call-done = bf16[1,8192,256]{2,1,0:T(8,128)(2,1)} async-done(((bf16[1,1024,256]{2,1,0:T(8,128)(2,1)}), bf16[1,8192,256]{2,1,0:T(8,128)(2,1)}) %all-gather.9.cloned.1.call-update) | async-done | bytes 4194320 | tf_op jit(solution)/shard_map/all_gather | solution.py:51
  96.4 62.7 %while.14 = (s32[]{:T(128)}, f32[128,16,128]{2,0,1:T(8,128)S(1)}, f32[128,16]{0,1:T(8,128)S(1)}, f32[128,16]{0,1:T(8,128)S(1)}, s32[8]{0:T(128)S(1)}, /*index=5*...) while((s32[]{:T(128)}, f32[128,16,128]{2,0,1:T(8,128)S(1)}, ...), condition=%wide.region_10.11_spmd, body=%wide.region_7.10_spmd.sunk | while | flops 1091047424 | bytes 28442832 | solution.py:76
  97.7 2.2 bitcast_reduce_fusion.2
  99.9 1.4 fusion.68
  101.3 2.9 %fusion.69 = f32[128,16,128]{2,0,1:T(8,128)S(1)} fusion(f32[1024,128,16]{1,0,2:T(8,128)S(1)} %get-tuple-element.135, f32[128,16]{0,1:T(8,128)S(1)} %max.4, f32[128,16,128]{2,0,1:T(8,128)S(1)} %get-tuple-element.152, f32[128,16]{0,1:T(8,128)S(1)} %get-tuple-element.137, bf16[8192,256]{1,0:T(8,128)(2,1)} %get-tuple-element.168, s32[]{:T(128)S(6)} %select_n.46, ...), kind=kOutput, calls=%fused_computation.8.clone.1 | convolution fusion | flops 543686656 | bytes 10764296 | tf_op jit(solution)/shard_map/while/body/eval_jaxpr/thp,pd->thd/dot_general | solution.py:68
  105.5 2.2 bitcast_reduce_fusion.2
  107.8 1.4 fusion.68
  109.2 2.9 %fusion.69 = f32[128,16,128]{2,0,1:T(8,128)S(1)} fusion(f32[1024,128,16]{1,0,2:T(8,128)S(1)} %get-tuple-element.135, f32[128,16]{0,1:T(8,128)S(1)} %max.4, f32[128,16,128]{2,0,1:T(8,128)S(1)} %get-tuple-element.152, f32[128,16]{0,1:T(8,128)S(1)} %get-tuple-element.137, bf16[8192,256]{1,0:T(8,128)(2,1)} %get-tuple-element.168, s32[]{:T(128)S(6)} %select_n.46, ...), kind=kOutput, calls=%fused_computation.8.clone.1 | convolution fusion | flops 543686656 | bytes 10764296 | tf_op jit(solution)/shard_map/while/body/eval_jaxpr/thp,pd->thd/dot_general | solution.py:68
  113.4 2.2 bitcast_reduce_fusion.2
  115.6 1.4 fusion.68
  117.0 2.9 %fusion.69 = f32[128,16,128]{2,0,1:T(8,128)S(1)} fusion(f32[1024,128,16]{1,0,2:T(8,128)S(1)} %get-tuple-element.135, f32[128,16]{0,1:T(8,128)S(1)} %max.4, f32[128,16,128]{2,0,1:T(8,128)S(1)} %get-tuple-element.152, f32[128,16]{0,1:T(8,128)S(1)} %get-tuple-element.137, bf16[8192,256]{1,0:T(8,128)(2,1)} %get-tuple-element.168, s32[]{:T(128)S(6)} %select_n.46, ...), kind=kOutput, calls=%fused_computation.8.clone.1 | convolution fusion | flops 543686656 | bytes 10764296 | tf_op jit(solution)/shard_map/while/body/eval_jaxpr/thp,pd->thd/dot_general | solution.py:68
  121.2 2.2 bitcast_reduce_fusion.2
  123.4 1.4 fusion.68
  124.8 2.9 %fusion.69 = f32[128,16,128]{2,0,1:T(8,128)S(1)} fusion(f32[1024,128,16]{1,0,2:T(8,128)S(1)} %get-tuple-element.135, f32[128,16]{0,1:T(8,128)S(1)} %max.4, f32[128,16,128]{2,0,1:T(8,128)S(1)} %get-tuple-element.152, f32[128,16]{0,1:T(8,128)S(1)} %get-tuple-element.137, bf16[8192,256]{1,0:T(8,128)(2,1)} %get-tuple-element.168, s32[]{:T(128)S(6)} %select_n.46, ...), kind=kOutput, calls=%fused_computation.8.clone.1 | convolution fusion | flops 543686656 | bytes 10764296 | tf_op jit(solution)/shard_map/while/body/eval_jaxpr/thp,pd->thd/dot_general | solution.py:68
  129.0 2.2 bitcast_reduce_fusion.2
  131.3 1.4 fusion.68
  132.7 2.9 %fusion.69 = f32[128,16,128]{2,0,1:T(8,128)S(1)} fusion(f32[1024,128,16]{1,0,2:T(8,128)S(1)} %get-tuple-element.135, f32[128,16]{0,1:T(8,128)S(1)} %max.4, f32[128,16,128]{2,0,1:T(8,128)S(1)} %get-tuple-element.152, f32[128,16]{0,1:T(8,128)S(1)} %get-tuple-element.137, bf16[8192,256]{1,0:T(8,128)(2,1)} %get-tuple-element.168, s32[]{:T(128)S(6)} %select_n.46, ...), kind=kOutput, calls=%fused_computation.8.clone.1 | convolution fusion | flops 543686656 | bytes 10764296 | tf_op jit(solution)/shard_map/while/body/eval_jaxpr/thp,pd->thd/dot_general | solution.py:68
  136.9 2.2 bitcast_reduce_fusion.2
  139.1 1.4 fusion.68
  140.5 2.9 %fusion.69 = f32[128,16,128]{2,0,1:T(8,128)S(1)} fusion(f32[1024,128,16]{1,0,2:T(8,128)S(1)} %get-tuple-element.135, f32[128,16]{0,1:T(8,128)S(1)} %max.4, f32[128,16,128]{2,0,1:T(8,128)S(1)} %get-tuple-element.152, f32[128,16]{0,1:T(8,128)S(1)} %get-tuple-element.137, bf16[8192,256]{1,0:T(8,128)(2,1)} %get-tuple-element.168, s32[]{:T(128)S(6)} %select_n.46, ...), kind=kOutput, calls=%fused_computation.8.clone.1 | convolution fusion | flops 543686656 | bytes 10764296 | tf_op jit(solution)/shard_map/while/body/eval_jaxpr/thp,pd->thd/dot_general | solution.py:68
  144.7 2.2 bitcast_reduce_fusion.2
  148.4 2.9 %fusion.69 = f32[128,16,128]{2,0,1:T(8,128)S(1)} fusion(f32[1024,128,16]{1,0,2:T(8,128)S(1)} %get-tuple-element.135, f32[128,16]{0,1:T(8,128)S(1)} %max.4, f32[128,16,128]{2,0,1:T(8,128)S(1)} %get-tuple-element.152, f32[128,16]{0,1:T(8,128)S(1)} %get-tuple-element.137, bf16[8192,256]{1,0:T(8,128)(2,1)} %get-tuple-element.168, s32[]{:T(128)S(6)} %select_n.46, ...), kind=kOutput, calls=%fused_computation.8.clone.1 | convolution fusion | flops 543686656 | bytes 10764296 | tf_op jit(solution)/shard_map/while/body/eval_jaxpr/thp,pd->thd/dot_general | solution.py:68
  152.6 2.2 bitcast_reduce_fusion.2
  156.2 2.9 %fusion.69 = f32[128,16,128]{2,0,1:T(8,128)S(1)} fusion(f32[1024,128,16]{1,0,2:T(8,128)S(1)} %get-tuple-element.135, f32[128,16]{0,1:T(8,128)S(1)} %max.4, f32[128,16,128]{2,0,1:T(8,128)S(1)} %get-tuple-element.152, f32[128,16]{0,1:T(8,128)S(1)} %get-tuple-element.137, bf16[8192,256]{1,0:T(8,128)(2,1)} %get-tuple-element.168, s32[]{:T(128)S(6)} %select_n.46, ...), kind=kOutput, calls=%fused_computation.8.clone.1 | convolution fusion | flops 543686656 | bytes 10764296 | tf_op jit(solution)/shard_map/while/body/eval_jaxpr/thp,pd->thd/dot_general | solution.py:68
  161.9 4.8 %fusion.51 = (f32[128]{0:T(128)S(1)}, f32[128,2048]{1,0:T(8,128)S(1)}) fusion(bf16[128,2048]{0,1:T(8,128)(2,1)S(1)} %bitcast.88, bf16[2048,2048]{1,0:T(8,128)(2,1)} %param.25, bf16[1,128,2048]{2,1,0:T(8,128)(2,1)S(1)} %copy-done.1), kind=kOutput, calls=%fused_computation.76 | convolution fusion | flops 1074528128 | bytes 10486272 | tf_op jit(solution)/shard_map/dot_general | solution.py:120
  168.2 45.8 %all-gather.7.cloned.1.call-done = bf16[1024,2048]{1,0:T(8,128)(2,1)} async-done(((bf16[128,2048]{1,0:T(8,128)(2,1)}), bf16[1024,2048]{1,0:T(8,128)(2,1)}) %all-gather.7.cloned.1.call-update) | async-done | bytes 4194320 | tf_op jit(solution)/shard_map/all_gather | solution.py:124
  214.0 15.1 %convolution_convert_fusion = bf16[1024,2048]{1,0:T(8,128)(2,1)} fusion(bf16[1024,2048]{1,0:T(8,128)(2,1)} %param.29, bf16[1024,2048]{1,0:T(8,128)(2,1)} %all-gather.7.cloned.1.call-done, bf16[2048,1024]{1,0:T(8,128)(2,1)} %param.28), kind=kOutput, calls=%fused_computation.25 | convolution fusion | flops 8601468928 | bytes 16777216 | tf_op jit(solution)/shard_map/dot_general | solution.py:131
  232.2 45.8 %reduce-scatter.2.cloned.1.call-done = bf16[128,2048]{1,0:T(8,128)(2,1)} async-done(((bf16[1024,2048]{1,0:T(8,128)(2,1)}), bf16[128,2048]{1,0:T(8,128)(2,1)}) %reduce-scatter.2.cloned.1.call-update) | async-done | bytes 524304 | tf_op jit(solution)/shard_map/reduce_scatter | solution.py:130
  278.0 2.0 fusion.39
  (79 shorter events, 20.9 us)
Async XLA Ops:
  6.5 50.4 %copy-start = (bf16[2048,256]{1,0:T(8,128)(2,1)S(1)}, bf16[2048,256]{1,0:T(8,128)(2,1)}, u32[]{:S(2)}) copy-start(bf16[2048,256]{1,0:T(8,128)(2,1)} %param.24) | copy-start | bytes 3145732
  6.5 40.7 %all-gather.5.cloned.1.call-start = ((), (), s32[]{:S(2)}) async-start(), calls=%async_computation.1 | async-start | bytes 2621440 | tf_op jit(solution)/shard_map/all_gather | solution.py:110
  7.3 89.2 %all-gather.9.cloned.1.call-start = ((), (), s32[]{:S(2)}) async-start(), calls=%async_computation.4 | async-start | bytes 4718592 | tf_op jit(solution)/shard_map/all_gather | solution.py:51
  49.1 164.9 %all-gather.7.cloned.1.call-start = ((), (), s32[]{:S(2)}) async-start(), calls=%async_computation.2 | async-start | bytes 4718592 | tf_op jit(solution)/shard_map/all_gather | solution.py:124
  51.7 5.2 %copy-start.1 = (bf16[1,128,2048]{2,1,0:T(8,128)(2,1)S(1)}, bf16[1,128,2048]{2,1,0:T(8,128)(2,1)}, u32[]{:S(2)}) copy-start(bf16[1,128,2048]{2,1,0:T(8,128)(2,1)} %param.16) | copy-start | bytes 1572868
  51.7 5.2 %copy-start.4 = (f32[2048]{0:T(1024)S(1)}, f32[2048]{0:T(1024)}, u32[]{:S(2)}) copy-start(f32[2048]{0:T(1024)} %param.22) | copy-start | bytes 24580
  51.8 5.2 %copy-start.5 = (f32[2048]{0:T(1024)S(1)}, f32[2048]{0:T(1024)}, u32[]{:S(2)}) copy-start(f32[2048]{0:T(1024)} %param.21) | copy-start | bytes 24580
  161.8 5.1 %copy-start.2 = (f32[2048]{0:T(1024)S(1)}, f32[2048]{0:T(1024)}, u32[]{:S(2)}) copy-start(f32[2048]{0:T(1024)} %param.27) | copy-start | bytes 24580
  161.9 5.1 %copy-start.3 = (f32[2048]{0:T(1024)S(1)}, f32[2048]{0:T(1024)}, u32[]{:S(2)}) copy-start(f32[2048]{0:T(1024)} %param.26) | copy-start | bytes 24580
  168.0 110.1 %reduce-scatter.2.cloned.1.call-start = ((), (), s32[]{:S(2)}) async-start(), calls=%async_computation.3 | async-start | bytes 4718592 | tf_op jit(solution)/shard_map/reduce_scatter | solution.py:130
  229.1 0.7 copy-start.6
  229.1 1.3 copy-start.7
Sparse Core Ops, SparseCore 0:
  9.2 38.0 all-gather.4
  49.3 47.1 all-gather.8
  168.1 45.8 all-gather.6
  229.3 48.7 reduce-scatter.1
where the time goes:
time: 288 us; the launch traced here: 287 us
  waiting for transfers between devices  167 us (58%)
  matrix products  67.1 us (23%)
  other arithmetic  22.2 us (8%)
  between operations  15.2 us (5%)
  local copies, waits for them, and re-layouts  8.7 us (3%)
  loops' own time  5.68 us (2%)
    reduce_scatter x1, waiting for transfers between devices, shards(): lax.psum_scatter(jnp.dot(hidden, contract_weight, preferred_element_type=...  45.8 us
    all_gather x1, waiting for transfers between devices, shards(): lax.all_gather(second, 'member', axis=0, tiled=True)  45.8 us
    all_gather x1, waiting for transfers between devices, folded_attention(): portion = lax.all_gather(selected, 'member', axis=0, tiled=True)  38.3 us
    all_gather x1, waiting for transfers between devices, shards(): every_block = lax.all_gather(prefix_cache, 'group', axis=0, tiled=True)  36.7 us
    dot_general x8, matrix products, advance(): jnp.einsum('thp,pd->thd', exponent.astype(jnp.bfloat16), key_block[:, hea...  23.5 us
    dot_general x8, matrix products, advance(): jnp.einsum('thd,pd->thp', queries, key_block[:, :head_size], preferred_el...  17.7 us
    dot_general x1, matrix products, shards(): jnp.dot(hidden, contract_weight, preferred_element_type=jnp.float32)  15.1 us
    reduce_sum x8, other arithmetic, advance(): denominator_next = denominator_now * rescale + jnp.sum(exponent, axis=-1)  11 us
  transfers between devices with their start and end apart: 4, of which 4 were waited for; matrix products, arithmetic and copies ran while one was open for 4% of the time, Pallas kernels for 0%

commit v1 on v0

--- a/solution.py
+++ b/solution.py
@@ -6,6 +6,22 @@
 
 EPSILON = 1e-05
 NEGATIVE = -1e30
+
+
+def lift_rings(local, device_axis, which_dim):
+    devs = lax.axis_size(device_axis)
+    runs = tuple(((ii, (ii + 1) % devs) for ii in range(devs)))
+
+    def test_cubes(arr_next):
+        if len(arr_next) == devs:
+            return arr_next
+        answer = lax.ppermute(arr_next[0], axis_name=device_axis, perm=runs)
+        return test_cubes([answer, *arr_next])
+
+    f_next = test_cubes([local])
+    local_out = jnp.concatenate(f_next, which_dim)
+    w2 = lax.axis_index(device_axis)
+    return jnp.roll(local_out, (w2 + 1) * local.shape[which_dim], which_dim)
 
 
 def layer_norm(values, gain, bias):
@@ -107,7 +123,7 @@
     row_count = tokens.shape[0]
     head_size = prefix_cache.shape[2] // 2
     head_count = tokens.shape[1] // head_size
-    every_block = lax.all_gather(prefix_cache, "group", axis=0, tiled=True)
+    every_block = lift_rings(prefix_cache, "group", 0)
     selected = lax.dynamic_index_in_dim(every_block, owner_here, 0, keepdims=False)
     tokens_wide = tokens.astype(jnp.float32)
     normed = layer_norm(tokens_wide, first_gain, first_bias).astype(jnp.bfloat16)

time: 288 us -> 292 us (1.014)
  starting transfers between devices: 0.31 us -> 3.96 us
    all_gather x1 -> x0, waiting for transfers between devices: 36.7 us -> none  [shards(): every_block = lax.all_gather(prefix_cache, 'group', axis=0, tiled=True)]
    ppermute x0 -> x3, waiting for transfers between devices: none -> 36.2 us  [test_cubes(): answer = lax.ppermute(arr_next[0], axis_name=device_axis, perm=runs)]
    ppermute x0 -> x3, starting transfers between devices: none -> 3.7 us  [test_cubes(): answer = lax.ppermute(arr_next[0], axis_name=device_axis, perm=runs)]
    unnamed x16 -> x27, local copies, waits for them, and re-layouts: 0.66 us -> 3.8 us
  transfers between devices with their start and end apart: 4 -> 6, of which waited for: 4 -> 6; matrix products, arithmetic and copies ran while one was open for 4% -> 4% of each run, Pallas kernels for 0% -> 0%
where the time goes in v1:
time: 292 us; the launch traced here: 291 us
  waiting for transfers between devices  168 us (58%)
  matrix products  66.9 us (23%)
  other arithmetic  20.1 us (7%)
  between operations  15.3 us (5%)
  local copies, waits for them, and re-layouts  10.8 us (4%)
  loops' own time  5.68 us (2%)
  starting transfers between devices  3.96 us (1%)
    reduce_scatter x1, waiting for transfers between devices, shards(): lax.psum_scatter(jnp.dot(hidden, contract_weight, preferred_element_type=...  45.8 us
    all_gather x1, waiting for transfers between devices, shards(): lax.all_gather(second, 'member', axis=0, tiled=True)  45.8 us
    all_gather x1, waiting for transfers between devices, folded_attention(): portion = lax.all_gather(selected, 'member', axis=0, tiled=True)  40.5 us
    ppermute x3, waiting for transfers between devices, test_cubes(): answer = lax.ppermute(arr_next[0], axis_name=device_axis, perm=runs)  36.2 us
    dot_general x8, matrix products, advance(): jnp.einsum('thp,pd->thd', exponent.astype(jnp.bfloat16), key_block[:, hea...  23.5 us
    dot_general x8, matrix products, advance(): jnp.einsum('thd,pd->thp', queries, key_block[:, :head_size], preferred_el...  17.7 us
    dot_general x1, matrix products, shards(): jnp.dot(hidden, contract_weight, preferred_element_type=jnp.float32)  15.1 us
    reduce_sum x8, other arithmetic, advance(): denominator_next = denominator_now * rescale + jnp.sum(exponent, axis=-1)  11 us
  transfers between devices with their start and end apart: 6, of which 6 were waited for; matrix products, arithmetic and copies ran while one was open for 4% of the time, Pallas kernels for 0%

profile of v1, /device:TPU:0, one launch (start us, length us, event | category | flops | bytes accessed | tf_op | source)
XLA Modules:
  0.0 291.1 jit_solution(15406287768047057123)
XLA Ops:
  6.5 2.9 %collective-permute-start = (bf16[1,1024,256]{2,1,0:T(8,128)(2,1)}, bf16[1,1024,256]{2,1,0:T(8,128)(2,1)S(1)}, u32[]{:S(2)}, u32[]{:S(2)}) collective-permute-start(bf16[1,1024,256]{2,1,0:T(8,128)(2,1)} %param.20), channel_id=1, source_target_pairs={{0,8},{8,16},{16,24},{24,0},{1,9},{9,17},{17,25},{25,1},{2,10},{10... | collective-permute-start | bytes 1572872 | tf_op jit(solution)/shard_map/ppermute | solution.py:18
  9.5 13.1 %collective-permute-done = bf16[1,1024,256]{2,1,0:T(8,128)(2,1)S(1)} collective-permute-done((bf16[1,1024,256]{2,1,0:T(8,128)(2,1)}, bf16[1,1024,256]{2,1,0:T(8,128)(2,1)S(1)}, u32[]{:S(2)}, u32[]{:S(2)}) %collective-permute-start) | collective-permute-done | bytes 524320 | tf_op jit(solution)/shard_map/ppermute | solution.py:18
  23.4 13.3 %collective-permute-done.1 = bf16[1,1024,256]{2,1,0:T(8,128)(2,1)S(1)} collective-permute-done((bf16[1,1024,256]{2,1,0:T(8,128)(2,1)S(1)}, bf16[1,1024,256]{2,1,0:T(8,128)(2,1)S(1)}, u32[]{:S(2)}, u32[]{:S(2)}) %collective-permute-start.1) | collective-permute-done | bytes 524320 | tf_op jit(solution)/shard_map/ppermute | solution.py:18
  39.9 9.8 %collective-permute-done.2 = bf16[1,1024,256]{2,1,0:T(8,128)(2,1)S(1)} collective-permute-done((bf16[1,1024,256]{2,1,0:T(8,128)(2,1)S(1)}, bf16[1,1024,256]{2,1,0:T(8,128)(2,1)S(1)}, u32[]{:S(2)}, u32[]{:S(2)}) %collective-permute-start.2) | collective-permute-done | bytes 524320 | tf_op jit(solution)/shard_map/ppermute | solution.py:18
  54.4 4.7 %fusion.30 = bf16[16,16,8,128]{3,2,1,0:T(8,128)(2,1)S(1)} fusion(bf16[2048,2048]{1,0:T(8,128)(2,1)} %param.23, bf16[1,128,2048]{2,1,0:T(8,128)(2,1)S(1)} %copy-done.1, f32[2048]{0:T(1024)S(1)} %copy-done.6, f32[2048]{0:T(1024)S(1)} %copy-done.7, f32[128]{0:T(128)S(1)} %add_rsqrt_fusion.1, f32[128]{0:T(128)S(1)} %broadcast_multiply_fusion.1), kind=kOutput, calls=%fused_computation.39 | convolution fusion | flops 1075576832 | bytes 9454592 | tf_op jit(solution)/shard_map/dot_general | solution.py:130
  60.5 40.5 %all-gather.6.cloned.1.call-done = bf16[1,8192,256]{2,1,0:T(8,128)(2,1)} async-done(((bf16[1,1024,256]{2,1,0:T(8,128)(2,1)}), bf16[1,8192,256]{2,1,0:T(8,128)(2,1)}) %all-gather.6.cloned.1.call-update) | async-done | bytes 4194320 | tf_op jit(solution)/shard_map/all_gather | solution.py:67
  101.0 62.7 %while.14 = (s32[]{:T(128)}, f32[128,16,128]{2,0,1:T(8,128)S(1)}, f32[128,16]{0,1:T(8,128)S(1)}, f32[128,16]{0,1:T(8,128)S(1)}, s32[8]{0:T(128)S(1)}, /*index=5*...) while((s32[]{:T(128)}, f32[128,16,128]{2,0,1:T(8,128)S(1)}, ...), condition=%wide.region_10.11_spmd, body=%wide.region_7.10_spmd.sunk | while | flops 1091047424 | bytes 28442832 | solution.py:92
  102.2 2.2 bitcast_reduce_fusion.2
  104.4 1.4 fusion.68
  105.8 2.9 %fusion.69 = f32[128,16,128]{2,0,1:T(8,128)S(1)} fusion(f32[1024,128,16]{1,0,2:T(8,128)S(1)} %get-tuple-element.128, f32[128,16]{0,1:T(8,128)S(1)} %max.4, f32[128,16,128]{2,0,1:T(8,128)S(1)} %get-tuple-element.145, f32[128,16]{0,1:T(8,128)S(1)} %get-tuple-element.130, bf16[8192,256]{1,0:T(8,128)(2,1)} %get-tuple-element.161, s32[]{:T(128)S(6)} %select_n.67, ...), kind=kOutput, calls=%fused_computation.8.clone.1 | convolution fusion | flops 543686656 | bytes 10764296 | tf_op jit(solution)/shard_map/while/body/eval_jaxpr/thp,pd->thd/dot_general | solution.py:84
  110.0 2.2 bitcast_reduce_fusion.2
  112.3 1.4 fusion.68
  113.7 2.9 %fusion.69 = f32[128,16,128]{2,0,1:T(8,128)S(1)} fusion(f32[1024,128,16]{1,0,2:T(8,128)S(1)} %get-tuple-element.128, f32[128,16]{0,1:T(8,128)S(1)} %max.4, f32[128,16,128]{2,0,1:T(8,128)S(1)} %get-tuple-element.145, f32[128,16]{0,1:T(8,128)S(1)} %get-tuple-element.130, bf16[8192,256]{1,0:T(8,128)(2,1)} %get-tuple-element.161, s32[]{:T(128)S(6)} %select_n.67, ...), kind=kOutput, calls=%fused_computation.8.clone.1 | convolution fusion | flops 543686656 | bytes 10764296 | tf_op jit(solution)/shard_map/while/body/eval_jaxpr/thp,pd->thd/dot_general | solution.py:84
  117.9 2.2 bitcast_reduce_fusion.2
  120.1 1.4 fusion.68
  121.5 2.9 %fusion.69 = f32[128,16,128]{2,0,1:T(8,128)S(1)} fusion(f32[1024,128,16]{1,0,2:T(8,128)S(1)} %get-tuple-element.128, f32[128,16]{0,1:T(8,128)S(1)} %max.4, f32[128,16,128]{2,0,1:T(8,128)S(1)} %get-tuple-element.145, f32[128,16]{0,1:T(8,128)S(1)} %get-tuple-element.130, bf16[8192,256]{1,0:T(8,128)(2,1)} %get-tuple-element.161, s32[]{:T(128)S(6)} %select_n.67, ...), kind=kOutput, calls=%fused_computation.8.clone.1 | convolution fusion | flops 543686656 | bytes 10764296 | tf_op jit(solution)/shard_map/while/body/eval_jaxpr/thp,pd->thd/dot_general | solution.py:84
  125.7 2.2 bitcast_reduce_fusion.2
  129.4 2.9 %fusion.69 = f32[128,16,128]{2,0,1:T(8,128)S(1)} fusion(f32[1024,128,16]{1,0,2:T(8,128)S(1)} %get-tuple-element.128, f32[128,16]{0,1:T(8,128)S(1)} %max.4, f32[128,16,128]{2,0,1:T(8,128)S(1)} %get-tuple-element.145, f32[128,16]{0,1:T(8,128)S(1)} %get-tuple-element.130, bf16[8192,256]{1,0:T(8,128)(2,1)} %get-tuple-element.161, s32[]{:T(128)S(6)} %select_n.67, ...), kind=kOutput, calls=%fused_computation.8.clone.1 | convolution fusion | flops 543686656 | bytes 10764296 | tf_op jit(solution)/shard_map/while/body/eval_jaxpr/thp,pd->thd/dot_general | solution.py:84
  133.6 2.2 bitcast_reduce_fusion.2
  137.2 2.9 %fusion.69 = f32[128,16,128]{2,0,1:T(8,128)S(1)} fusion(f32[1024,128,16]{1,0,2:T(8,128)S(1)} %get-tuple-element.128, f32[128,16]{0,1:T(8,128)S(1)} %max.4, f32[128,16,128]{2,0,1:T(8,128)S(1)} %get-tuple-element.145, f32[128,16]{0,1:T(8,128)S(1)} %get-tuple-element.130, bf16[8192,256]{1,0:T(8,128)(2,1)} %get-tuple-element.161, s32[]{:T(128)S(6)} %select_n.67, ...), kind=kOutput, calls=%fused_computation.8.clone.1 | convolution fusion | flops 543686656 | bytes 10764296 | tf_op jit(solution)/shard_map/while/body/eval_jaxpr/thp,pd->thd/dot_general | solution.py:84
  141.4 2.2 bitcast_reduce_fusion.2
  145.0 2.9 %fusion.69 = f32[128,16,128]{2,0,1:T(8,128)S(1)} fusion(f32[1024,128,16]{1,0,2:T(8,128)S(1)} %get-tuple-element.128, f32[128,16]{0,1:T(8,128)S(1)} %max.4, f32[128,16,128]{2,0,1:T(8,128)S(1)} %get-tuple-element.145, f32[128,16]{0,1:T(8,128)S(1)} %get-tuple-element.130, bf16[8192,256]{1,0:T(8,128)(2,1)} %get-tuple-element.161, s32[]{:T(128)S(6)} %select_n.67, ...), kind=kOutput, calls=%fused_computation.8.clone.1 | convolution fusion | flops 543686656 | bytes 10764296 | tf_op jit(solution)/shard_map/while/body/eval_jaxpr/thp,pd->thd/dot_general | solution.py:84
  149.3 2.2 bitcast_reduce_fusion.2
  152.9 2.9 %fusion.69 = f32[128,16,128]{2,0,1:T(8,128)S(1)} fusion(f32[1024,128,16]{1,0,2:T(8,128)S(1)} %get-tuple-element.128, f32[128,16]{0,1:T(8,128)S(1)} %max.4, f32[128,16,128]{2,0,1:T(8,128)S(1)} %get-tuple-element.145, f32[128,16]{0,1:T(8,128)S(1)} %get-tuple-element.130, bf16[8192,256]{1,0:T(8,128)(2,1)} %get-tuple-element.161, s32[]{:T(128)S(6)} %select_n.67, ...), kind=kOutput, calls=%fused_computation.8.clone.1 | convolution fusion | flops 543686656 | bytes 10764296 | tf_op jit(solution)/shard_map/while/body/eval_jaxpr/thp,pd->thd/dot_general | solution.py:84
  157.1 2.2 bitcast_reduce_fusion.2
  159.3 1.4 fusion.68
  160.7 2.9 %fusion.69 = f32[128,16,128]{2,0,1:T(8,128)S(1)} fusion(f32[1024,128,16]{1,0,2:T(8,128)S(1)} %get-tuple-element.128, f32[128,16]{0,1:T(8,128)S(1)} %max.4, f32[128,16,128]{2,0,1:T(8,128)S(1)} %get-tuple-element.145, f32[128,16]{0,1:T(8,128)S(1)} %get-tuple-element.130, bf16[8192,256]{1,0:T(8,128)(2,1)} %get-tuple-element.161, s32[]{:T(128)S(6)} %select_n.67, ...), kind=kOutput, calls=%fused_computation.8.clone.1 | convolution fusion | flops 543686656 | bytes 10764296 | tf_op jit(solution)/shard_map/while/body/eval_jaxpr/thp,pd->thd/dot_general | solution.py:84
  166.4 4.8 %fusion.51 = (f32[128]{0:T(128)S(1)}, f32[128,2048]{1,0:T(8,128)S(1)}) fusion(bf16[128,2048]{0,1:T(8,128)(2,1)S(1)} %bitcast.88, bf16[2048,2048]{1,0:T(8,128)(2,1)} %param.25, bf16[1,128,2048]{2,1,0:T(8,128)(2,1)S(1)} %copy-done.1), kind=kOutput, calls=%fused_computation.84 | convolution fusion | flops 1074528128 | bytes 10486272 | tf_op jit(solution)/shard_map/dot_general | solution.py:136
  172.8 45.8 %all-gather.4.cloned.1.call-done = bf16[1024,2048]{1,0:T(8,128)(2,1)} async-done(((bf16[128,2048]{1,0:T(8,128)(2,1)}), bf16[1024,2048]{1,0:T(8,128)(2,1)}) %all-gather.4.cloned.1.call-update) | async-done | bytes 4194320 | tf_op jit(solution)/shard_map/all_gather | solution.py:140
  218.6 15.1 %convolution_convert_fusion = bf16[1024,2048]{1,0:T(8,128)(2,1)} fusion(bf16[1024,2048]{1,0:T(8,128)(2,1)} %param.29, bf16[1024,2048]{1,0:T(8,128)(2,1)} %all-gather.4.cloned.1.call-done, bf16[2048,1024]{1,0:T(8,128)(2,1)} %param.28), kind=kOutput, calls=%fused_computation.25 | convolution fusion | flops 8601468928 | bytes 16777216 | tf_op jit(solution)/shard_map/dot_general | solution.py:147
  236.8 45.8 %reduce-scatter.2.cloned.1.call-done = bf16[128,2048]{1,0:T(8,128)(2,1)} async-done(((bf16[1024,2048]{1,0:T(8,128)(2,1)}), bf16[128,2048]{1,0:T(8,128)(2,1)}) %reduce-scatter.2.cloned.1.call-update) | async-done | bytes 524304 | tf_op jit(solution)/shard_map/reduce_scatter | solution.py:146
  282.6 2.0 fusion.39
  (94 shorter events, 25.6 us)
Async XLA Ops:
  6.5 52.7 %copy-start = (bf16[2048,256]{1,0:T(8,128)(2,1)S(1)}, bf16[2048,256]{1,0:T(8,128)(2,1)}, u32[]{:S(2)}) copy-start(bf16[2048,256]{1,0:T(8,128)(2,1)} %param.24) | copy-start | bytes 3145732
  6.5 46.4 %copy-start.2 = (bf16[1,1024,256]{2,1,0:T(8,128)(2,1)S(1)}, bf16[1,1024,256]{2,1,0:T(8,128)(2,1)}, u32[]{:S(2)}) copy-start(bf16[1,1024,256]{2,1,0:T(8,128)(2,1)} %param.20) | copy-start | bytes 1572868
  6.5 94.4 %all-gather.6.cloned.1.call-start = ((), (), s32[]{:S(2)}) async-start(), calls=%async_computation.3 | async-start | bytes 4718592 | tf_op jit(solution)/shard_map/all_gather | solution.py:67
  6.5 16.1 %collective-permute-start = (bf16[1,1024,256]{2,1,0:T(8,128)(2,1)}, bf16[1,1024,256]{2,1,0:T(8,128)(2,1)S(1)}, u32[]{:S(2)}, u32[]{:S(2)}) collective-permute-start(bf16[1,1024,256]{2,1,0:T(8,128)(2,1)} %param.20), channel_id=1, source_target_pairs={{0,8},{8,16},{16,24},{24,0},{1,9},{9,17},{17,25},{25,1},{2,10},{10... | collective-permute-start | bytes 1572872 | tf_op jit(solution)/shard_map/ppermute | solution.py:18
  22.6 14.0 %collective-permute-start.1 = (bf16[1,1024,256]{2,1,0:T(8,128)(2,1)S(1)}, bf16[1,1024,256]{2,1,0:T(8,128)(2,1)S(1)}, u32[]{:S(2)}, u32[]{:S(2)}) collective-permute-start(bf16[1,1024,256]{2,1,0:T(8,128)(2,1)S(1)} %collective-permute-done), channel_id=1, source_target_pairs={{0,8},{8,16},{16,24},{24,0},{1,9},{9,17},{17,25},{25,1},{2,10},{10... | collective-permute-start | bytes 1572872 | tf_op jit(solution)/shard_map/ppermute | solution.py:18
  36.6 13.1 %collective-permute-start.2 = (bf16[1,1024,256]{2,1,0:T(8,128)(2,1)S(1)}, bf16[1,1024,256]{2,1,0:T(8,128)(2,1)S(1)}, u32[]{:S(2)}, u32[]{:S(2)}) collective-permute-start(bf16[1,1024,256]{2,1,0:T(8,128)(2,1)S(1)} %collective-permute-done.1), channel_id=1, source_target_pairs={{0,8},{8,16},{16,24},{24,0},{1,9},{9,17},{17,25},{25,1},{2,10},{10... | collective-permute-start | bytes 1572872 | tf_op jit(solution)/shard_map/ppermute | solution.py:18
  49.7 0.8 copy-start.3
  50.5 3.3 %copy-start.1 = (bf16[1,128,2048]{2,1,0:T(8,128)(2,1)S(1)}, bf16[1,128,2048]{2,1,0:T(8,128)(2,1)}, u32[]{:S(2)}) copy-start(bf16[1,128,2048]{2,1,0:T(8,128)(2,1)} %param.16) | copy-start | bytes 1572868
  50.6 3.8 %copy-start.6 = (f32[2048]{0:T(1024)S(1)}, f32[2048]{0:T(1024)}, u32[]{:S(2)}) copy-start(f32[2048]{0:T(1024)} %param.22) | copy-start | bytes 24580
  50.6 3.8 %copy-start.7 = (f32[2048]{0:T(1024)S(1)}, f32[2048]{0:T(1024)}, u32[]{:S(2)}) copy-start(f32[2048]{0:T(1024)} %param.21) | copy-start | bytes 24580
  53.8 164.8 %all-gather.4.cloned.1.call-start = ((), (), s32[]{:S(2)}) async-start(), calls=%async_computation.1 | async-start | bytes 4718592 | tf_op jit(solution)/shard_map/all_gather | solution.py:140
  166.4 5.1 %copy-start.4 = (f32[2048]{0:T(1024)S(1)}, f32[2048]{0:T(1024)}, u32[]{:S(2)}) copy-start(f32[2048]{0:T(1024)} %param.27) | copy-start | bytes 24580
  166.4 5.1 %copy-start.5 = (f32[2048]{0:T(1024)S(1)}, f32[2048]{0:T(1024)}, u32[]{:S(2)}) copy-start(f32[2048]{0:T(1024)} %param.26) | copy-start | bytes 24580
  172.5 110.1 %reduce-scatter.2.cloned.1.call-start = ((), (), s32[]{:S(2)}) async-start(), calls=%async_computation.2 | async-start | bytes 4718592 | tf_op jit(solution)/shard_map/reduce_scatter | solution.py:146
  233.7 0.7 copy-start.8
  233.7 1.3 copy-start.9
Sparse Core Ops, SparseCore 0:
  53.9 46.9 all-gather.5
  172.7 45.8 all-gather.3
  233.9 48.7 reduce-scatter.1
